TPU v7x, 32 devices: a whole 2x2x4 slice. The times are simulated.
32 devices in a mesh: dp: 32 (over z, y, x, core).
Axes of the slice: x: 2, y: 2, z: 4, core: 2. Of those that a mesh axis runs over, the one named last changes fastest.
Arguments:
- images: bfloat16 [64, 197, 384], P('dp'), may hold values from -6 to 6
- params: bfloat16 [1777664], P('dp'), may hold values from -1.2 to 1.4
- cotangent: bfloat16 [64, 197, 384], P('dp'), may hold values from -6 to 6
- counts: int32 [32], P('dp'), may hold values from 1 to 2, as said below
Outputs:
- block_out: bfloat16 [64, 197, 384], P('dp')
- image_grad: bfloat16 [64, 197, 384], P('dp')
- param_grad: float32 [1777664], P('dp')
Inputs may be any that keep to these rules, and one draw needn't show every extreme that they name: `counts`: every device has 1 to 2 live images; some device has exactly 2 and some exactly 1.
All inputs are finite; a program needn't handle non-finite values.
Results may differ from a plain program's by a relative error of at most 0.0075.
Values may be sent and summed in bfloat16 or wider, within the bound.
No kernel may reach another device: no remote copies, remote signals or barrier semaphores. Data moves between devices by JAX's collectives and lax.ppermute only.
A program may use at most 128 MiB of HBM per device.

v0:
```python
import jax
import jax.numpy as jnp
from jax import lax
from jax.sharding import PartitionSpec as P

D = 384
HEADS = 6
FF = 1536
TOK = 197
MB = 2
CAP = 1
EPSILON = 1e-06
SQRT_HALF = 0.7071067811865476
INV_ROOT_TAU = 0.3989422804014327


def param_layout():
    return [
        ("w_qkv", (D, 3 * D)),
        ("b_query", (D,)),
        ("b_value", (D,)),
        ("w_out", (D, D)),
        ("b_out", (D,)),
        ("w_up", (D, FF)),
        ("b_up", (FF,)),
        ("w_down", (FF, D)),
        ("b_down", (D,)),
        ("g_first", (D,)),
        ("b_first", (D,)),
        ("g_second", (D,)),
        ("b_second", (D,)),
    ]


def unpack_flat(flat_buffer):
    pieces = {}
    position = 0
    for entry_name, entry_shape in param_layout():
        entry_size = 1
        for extent_value in entry_shape:
            entry_size = entry_size * extent_value
        pieces[entry_name] = flat_buffer[position : position + entry_size].reshape(entry_shape)
        position = position + entry_size
    return pieces


def fetch_weights(params):
    return unpack_flat(lax.all_gather(params, "dp", axis=0, tiled=True))


def standardize(values):
    centre = values - jnp.mean(values, -1, keepdims=True)
    inverse = lax.rsqrt(jnp.mean(centre * centre, -1, keepdims=True) + EPSILON)
    return (centre * inverse, inverse)


def left_product(first, second):
    return lax.dot_general(
        first, second, (((0,), (0,)), ((), ())), preferred_element_type=jnp.float32
    )


def right_product(first, second):
    return lax.dot_general(
        first, second, (((1,), (1,)), ((), ())), preferred_element_type=jnp.float32
    )


def norm_back(grad_normed, normed_rows, inverse, gain):
    scaled = grad_normed * gain
    return inverse * (
        scaled
        - jnp.mean(scaled, -1, keepdims=True)
        - normed_rows * jnp.mean(scaled * normed_rows, -1, keepdims=True)
    )


def gelu_slope(values):
    return 0.5 * (1.0 + lax.erf(values * SQRT_HALF)) + values * INV_ROOT_TAU * jnp.exp(
        -0.5 * values * values
    )


def head_split(values, image_count):
    return values.reshape(image_count, TOK, HEADS, D // HEADS)


def as_float(values):
    return values.astype(jnp.float32)


def forward_pass(weights, image_block):
    image_count = image_block.shape[0]
    scale = float(D // HEADS) ** (-0.5)
    tokens_in = image_block.reshape(-1, D).astype(jnp.float32)
    first_hat, first_inv = standardize(tokens_in)
    normed = (first_hat * as_float(weights["g_first"]) + as_float(weights["b_first"])).astype(
        jnp.bfloat16
    )
    joined = jnp.dot(normed, weights["w_qkv"], preferred_element_type=jnp.float32)
    query = (joined[:, :D] + as_float(weights["b_query"])).astype(jnp.bfloat16)
    keys_all = joined[:, D : 2 * D].astype(jnp.bfloat16)
    values_all = (joined[:, 2 * D :] + as_float(weights["b_value"])).astype(jnp.bfloat16)
    raw_scores = (
        jnp.einsum(
            "bqhd,bkhd->bhqk",
            head_split(query, image_count),
            head_split(keys_all, image_count),
            preferred_element_type=jnp.float32,
        )
        * scale
    )
    peak = jnp.max(raw_scores, -1, keepdims=True)
    log_total = peak + jnp.log(jnp.sum(jnp.exp(raw_scores - peak), -1, keepdims=True))
    probs_low = jnp.exp(raw_scores - log_total).astype(jnp.bfloat16)
    mixed = (
        jnp.einsum(
            "bhqk,bkhd->bqhd",
            probs_low,
            head_split(values_all, image_count),
            preferred_element_type=jnp.float32,
        )
        .reshape(-1, D)
        .astype(jnp.bfloat16)
    )
    middle = tokens_in + (
        jnp.dot(mixed, weights["w_out"], preferred_element_type=jnp.float32)
        + as_float(weights["b_out"])
    )
    second_hat, second_inv = standardize(middle)
    second = (second_hat * as_float(weights["g_second"]) + as_float(weights["b_second"])).astype(
        jnp.bfloat16
    )
    hidden_pre = jnp.dot(second, weights["w_up"], preferred_element_type=jnp.float32) + as_float(
        weights["b_up"]
    )
    hidden = jax.nn.gelu(hidden_pre, approximate=False).astype(jnp.bfloat16)
    result = middle + (
        jnp.dot(hidden, weights["w_down"], preferred_element_type=jnp.float32)
        + as_float(weights["b_down"])
    )
    saved = (
        first_hat,
        first_inv,
        normed,
        query,
        keys_all,
        values_all,
        log_total,
        mixed,
        second_hat,
        second_inv,
        second,
        hidden_pre,
        hidden,
    )
    return (result.astype(jnp.bfloat16).reshape(image_block.shape), saved)


def backward_pass(weights, saved, grad_out):
    (
        first_hat,
        first_inv,
        normed,
        query,
        keys_all,
        values_all,
        log_total,
        mixed,
        second_hat,
        second_inv,
        second,
        hidden_pre,
        hidden,
    ) = saved
    image_count = query.shape[0] // TOK
    scale = float(D // HEADS) ** (-0.5)
    grads = {}
    grad_low = grad_out.astype(jnp.bfloat16)
    grads["w_down"] = left_product(hidden, grad_low)
    grads["b_down"] = jnp.sum(as_float(grad_low), 0)
    grad_pre = (right_product(grad_low, weights["w_down"]) * gelu_slope(hidden_pre)).astype(
        jnp.bfloat16
    )
    grads["w_up"] = left_product(second, grad_pre)
    grads["b_up"] = jnp.sum(as_float(grad_pre), 0)
    grad_second = right_product(grad_pre, weights["w_up"])
    grads["g_second"] = jnp.sum(grad_second * second_hat, 0)
    grads["b_second"] = jnp.sum(grad_second, 0)
    grad_middle = grad_out + norm_back(
        grad_second, second_hat, second_inv, as_float(weights["g_second"])
    )
    grad_attn = grad_middle.astype(jnp.bfloat16)
    grads["w_out"] = left_product(mixed, grad_attn)
    grads["b_out"] = jnp.sum(as_float(grad_attn), 0)
    grad_mixed = head_split(
        right_product(grad_attn, weights["w_out"]).astype(jnp.bfloat16), image_count
    )
    query_heads = head_split(query, image_count)
    key_heads = head_split(keys_all, image_count)
    value_heads = head_split(values_all, image_count)
    raw_scores = (
        jnp.einsum("bqhd,bkhd->bhqk", query_heads, key_heads, preferred_element_type=jnp.float32)
        * scale
    )
    probs = jnp.exp(raw_scores - log_total)
    probs_low = probs.astype(jnp.bfloat16)
    grad_values = jnp.einsum(
        "bhqk,bqhd->bkhd", probs_low, grad_mixed, preferred_element_type=jnp.float32
    )
    grad_probs = jnp.einsum(
        "bqhd,bkhd->bhqk", grad_mixed, value_heads, preferred_element_type=jnp.float32
    )
    grad_scores = (probs * (grad_probs - jnp.sum(grad_probs * probs, -1, keepdims=True))).astype(
        jnp.bfloat16
    )
    grad_query = (
        jnp.einsum("bhqk,bkhd->bqhd", grad_scores, key_heads, preferred_element_type=jnp.float32)
        * scale
    )
    grad_keys = (
        jnp.einsum("bhqk,bqhd->bkhd", grad_scores, query_heads, preferred_element_type=jnp.float32)
        * scale
    )
    grad_joined = jnp.concatenate(
        [grad_query.reshape(-1, D), grad_keys.reshape(-1, D), grad_values.reshape(-1, D)], 1
    ).astype(jnp.bfloat16)
    grads["w_qkv"] = left_product(normed, grad_joined)
    joined_sums = jnp.sum(as_float(grad_joined), 0)
    grads["b_query"] = joined_sums[:D]
    grads["b_value"] = joined_sums[2 * D :]
    grad_first = right_product(grad_joined, weights["w_qkv"])
    grads["g_first"] = jnp.sum(grad_first * first_hat, 0)
    grads["b_first"] = jnp.sum(grad_first, 0)
    grad_in = grad_middle + norm_back(
        grad_first, first_hat, first_inv, as_float(weights["g_first"])
    )
    return (grads, grad_in.astype(jnp.bfloat16))


def on_device(images, params, cotangent, counts):
    full_length = params.shape[0] * lax.axis_size("dp")
    live_total = counts[0]
    totals = {}
    outputs = []
    in_grads = []
    weights = None
    for micro_step in range(MB):
        weights = fetch_weights(params)
        block_in = images[micro_step * CAP : (micro_step + 1) * CAP]
        result, saved = forward_pass(weights, block_in)
        outputs.append(result)
        weights = unpack_flat(lax.all_gather(params, "dp", axis=0, tiled=True))
        live = (micro_step * CAP + jnp.arange(CAP, dtype=jnp.int32) < live_total).astype(
            jnp.float32
        )
        grad_out = (
            cotangent[micro_step * CAP : (micro_step + 1) * CAP].astype(jnp.float32)
            * live[:, None, None]
        ).reshape(-1, D)
        grads, grad_in = backward_pass(weights, saved, grad_out)
        in_grads.append(grad_in.reshape(block_in.shape))
        for entry_name, entry_shape in param_layout():
            if micro_step == 0:
                totals[entry_name] = grads[entry_name]
            else:
                totals[entry_name] = totals[entry_name] + grads[entry_name]
    pieces = [totals[entry_name].reshape(-1) for entry_name, entry_shape in param_layout()]
    used_length = sum([piece_part.shape[0] for piece_part in pieces])
    pieces.append(jnp.zeros((full_length - used_length,), jnp.float32))
    flat_grad = jnp.concatenate(pieces)
    owned = lax.psum_scatter(flat_grad, "dp", scatter_dimension=0, tiled=True)
    return (jnp.concatenate(outputs, 0), jnp.concatenate(in_grads, 0), owned)


def solution(mesh):
    placed = (P("dp", None, None), P("dp"), P("dp", None, None), P("dp"))
    return jax.shard_map(
        on_device,
        mesh=mesh,
        in_specs=placed,
        out_specs=(P("dp", None, None), P("dp", None, None), P("dp")),
        check_vma=False,
    )
```

profile of v0, /device:TPU:0, one launch (start us, length us, event | category | flops | bytes accessed | tf_op | source)
XLA Modules:
  0.0 429.3 jit_solution(1542696043808574378)
XLA Ops:
  7.2 1.7 reshape.453
  9.7 1.6 fusion.136
  13.5 1.4 convert_reduce_fusion.6
  16.0 70.9 %all-gather.3.cloned.1.call-done = bf16[32,1,55552]{2,1,0:T(2,128)(2,1)} async-done(((bf16[1,1,55552]{2,1,0:T(2,128)(2,1)}), bf16[32,1,55552]{2,1,0:T(2,128)(2,1)}) %all-gather.3.cloned.1.call-update) | async-done | bytes 3555344 | tf_op jit(solution)/shard_map/all_gather | solution.py:48
  86.9 21.3 %reduce.14 = bf16[32,55552]{1,0:T(8,128)(2,1)S(1)} reduce(bf16[32,1,55552]{2,1,0:T(2,128)(2,1)} %all-gather.3.cloned.1.call-done, bf16[]{:T(256)} %constant.101), dimensions={1}, to_apply=%all-gather.reduce_sub_computation | reduce | bytes 7110658 | tf_op jit(solution)/shard_map/all_gather | solution.py:48
  108.2 7.0 %reshape.454 = bf16[1777664]{0:T(1024)(128)(2,1)} reshape(bf16[32,55552]{1,0:T(8,128)(2,1)S(1)} %reduce.14) | data formatting | bytes 7110656
  115.3 1.4 slice_convert_fusion.3
  116.7 1.7 slice.143
  118.4 1.3 slice_convert_fusion.2
  119.7 3.7 fusion.134
  123.4 1.0 reshape.423
  126.0 0.7 slice.190
  126.7 0.8 fusion.82
  128.7 1.2 reshape.427
  129.9 2.2 reshape.428
  133.6 1.5 reshape.429
  135.2 1.0 copy.60
  136.2 1.8 copy.61
  138.0 1.7 copy.62
  139.8 1.4 fusion.139
  142.8 3.8 fusion.7
  146.6 3.8 fusion.4
  150.4 1.4 convert_reduce_fusion.1
  151.9 1.2 multiply_reduce_fusion.3
  153.1 1.5 convert_reduce_fusion
  154.6 1.9 convert_reduce_fusion.9
  156.5 0.8 convert_reduce_fusion.8
  157.3 0.7 copy-done.10
  158.0 1.0 convolution_convert_fusion.4
  159.0 1.7 copy.75
  160.8 2.0 convolution_convert_fusion
  168.7 1.9 fusion.63
  171.5 1.2 fusion.131
  173.7 1.1 fusion.128
  175.8 1.8 convolution_add_fusion
  177.6 2.5 reshape.447
  180.1 3.0 constant_dynamic-update-slice_fusion.9
  183.1 1.3 constant_dynamic-update-slice_fusion.8
  184.4 1.3 constant_dynamic-update-slice_fusion.7
  185.7 1.1 convolution_add_fusion.5
  186.8 1.9 reshape.448
  188.8 3.1 convolution_add_fusion.2
  191.9 2.4 reshape.449
  194.3 1.8 fusion.125
  196.0 2.0 convolution_add_fusion.1
  198.1 3.3 reshape.450
  201.4 2.2 constant_dynamic-update-slice_fusion.6
  203.6 1.3 constant_dynamic-update-slice_fusion.5
  204.9 20.3 %dynamic-update-slice.5 = f32[1777664]{0:T(1024)} dynamic-update-slice(f32[1777664]{0:T(1024)} %constant_dynamic-update-slice_fusion.5, f32[589824]{0:T(1024)S(1)} %reshape.449, s32[]{} %constant.107) | dynamic-update-slice | bytes 4718596
  225.1 1.3 add_dynamic-update-slice_fusion
  226.5 21.2 %dynamic-update-slice.7 = f32[1777664]{0:T(1024)} dynamic-update-slice(f32[1777664]{0:T(1024)} %add_dynamic-update-slice_fusion, f32[589824]{0:T(1024)} %reshape.450, s32[]{} %constant.109) | dynamic-update-slice | bytes 4718596
  247.8 1.3 constant_dynamic-update-slice_fusion.4
  249.1 1.0 fusion.72
  250.1 1.3 constant_dynamic-update-slice_fusion.3
  251.4 1.3 constant_dynamic-update-slice_fusion.2
  252.8 1.3 constant_dynamic-update-slice_fusion.1
  254.1 1.3 constant_dynamic-update-slice_fusion
  255.4 1.3 broadcast_dynamic-update-slice_fusion
  256.8 1.2 copy-done.1
  258.0 1.6 fusion.39
  260.2 1.0 copy.79
  261.4 1.0 copy.80
  262.4 158.2 %all-reduce.3.cloned.1.call-done = f32[1777664]{0:T(1024)} async-done(((f32[1777664]{0:T(1024)}), f32[1777664]{0:T(1024)}) %all-reduce.3.cloned.1.call-update) | async-done | bytes 7110672
  420.5 1.8 dynamic-slice
  (240 shorter events, 18.5 us)
Async XLA Ops:
  7.2 79.8 %all-gather.3.cloned.1.call-start = ((), (), s32[]{:S(2)}) async-start(), calls=%async_computation | async-start | bytes 7332864 | tf_op jit(solution)/shard_map/all_gather | solution.py:48
  8.9 411.6 %all-reduce.3.cloned.1.call-start = ((), (), s32[]{:S(2)}) async-start(), calls=%async_computation.1 | async-start | bytes 14221312
  9.6 3.4 copy-start.47
  116.7 15.8 %copy-start.64 = (f32[384]{0:T(512)}, f32[384]{0:T(512)S(1)}, u32[]{:S(2)}) copy-start(f32[384]{0:T(512)S(1)} %get-tuple-element.43) | copy-start | bytes 4612
  119.7 3.7 slice-start
  124.4 1.6 copy-start.2
  127.7 4.4 %copy-start.29 = (bf16[197,384]{0,1:T(8,128)(2,1)}, bf16[197,384]{0,1:T(8,128)(2,1)S(1)}, u32[]{:S(2)}) copy-start(bf16[197,384]{0,1:T(8,128)(2,1)S(1)} %copy.65) | copy-start | bytes 453892
  128.4 1.5 copy-start.17
  132.1 1.6 copy-start.16
  132.4 2.7 copy-start.27
  132.8 2.3 copy-start.59
  136.2 5.2 %copy-start.31 = (bf16[197,384]{0,1:T(8,128)(2,1)}, bf16[197,384]{0,1:T(8,128)(2,1)S(1)}, u32[]{:S(2)}) copy-start(bf16[197,384]{0,1:T(8,128)(2,1)S(1)} %copy.60) | copy-start | bytes 453892
  141.4 1.3 copy-start.15
  141.4 1.3 copy-start.60
  141.4 1.3 copy-start.62
  141.4 1.3 copy-start.71
  141.5 1.3 copy-start.80
  142.5 12.0 %copy-start.69 = (f32[197]{0:T(256)}, f32[197]{0:T(256)S(1)}, u32[]{:S(2)}) copy-start(f32[197]{0:T(256)S(1)} %broadcast_multiply_fusion.10) | copy-start | bytes 2368
  142.7 11.8 %copy-start.73 = (f32[197]{0:T(256)}, f32[197]{0:T(256)S(1)}, u32[]{:S(2)}) copy-start(f32[197]{0:T(256)S(1)} %add_rsqrt_fusion.2) | copy-start | bytes 2368
  146.6 3.8 copy-start
  146.6 3.8 copy-start.44
  151.9 1.2 copy-start.48
  151.9 1.2 copy-start.42
  154.6 2.0 copy-start.20
  160.8 2.0 copy-start.30
  160.8 2.0 copy-start.33
  163.2 1.2 copy-start.37
  164.5 8.3 %copy-start.23 = (bf16[6,64,197]{2,1,0:T(8,128)(2,1)}, bf16[6,64,197]{2,1,0:T(8,128)(2,1)S(1)}, u32[]{:S(2)}) copy-start(bf16[6,64,197]{2,1,0:T(8,128)(2,1)S(1)} %fusion.35) | copy-start | bytes 453892
  164.7 8.0 %copy-start.25 = (bf16[6,64,197]{2,1,0:T(8,128)(2,1)}, bf16[6,64,197]{2,1,0:T(8,128)(2,1)S(1)}, u32[]{:S(2)}) copy-start(bf16[6,64,197]{2,1,0:T(8,128)(2,1)S(1)} %fusion.34) | copy-start | bytes 453892
  166.6 1.2 copy-start.41
  172.7 2.0 copy-start.49
  172.8 2.0 copy-start.63
  172.8 2.0 copy-start.70
  172.8 2.0 copy-start.74
  180.1 5.6 %copy-start.11 = (f32[197,384]{1,0:T(8,128)S(1)}, f32[197,384]{1,0:T(8,128)}, u32[]{:S(2)}) copy-start(f32[197,384]{1,0:T(8,128)} %copy-done.10) | copy-start | bytes 907780
  180.1 5.6 %copy-start.21 = (f32[384,384]{1,0:T(8,128)S(1)}, f32[384,384]{1,0:T(8,128)}, u32[]{:S(2)}) copy-start(f32[384,384]{1,0:T(8,128)} %fusion.128) | copy-start | bytes 1769476
  180.1 5.6 %copy-start.28 = (bf16[6,64,197]{2,1,0:T(8,128)(2,1)S(1)}, bf16[6,64,197]{2,1,0:T(8,128)(2,1)}, u32[]{:S(2)}) copy-start(bf16[6,64,197]{2,1,0:T(8,128)(2,1)} %copy-done.27) | copy-start | bytes 453892
  185.7 3.1 copy-start.61
  185.7 3.1 copy-start.72
  191.9 2.4 copy-start.45
  194.2 1.8 copy-start.19
  194.3 1.8 copy-start.43
  198.1 5.5 %copy-start.77 = (f32[384]{0:T(512)S(1)}, f32[384]{0:T(512)}, u32[]{:S(2)}) copy-start(f32[384]{0:T(512)} %get-tuple-element.32) | copy-start | bytes 4612
  198.1 5.5 %copy-start.83 = (f32[384]{0:T(512)S(1)}, f32[384]{0:T(512)}, u32[]{:S(2)}) copy-start(f32[384]{0:T(512)} %get-tuple-element.34) | copy-start | bytes 4612
  204.9 20.3 %copy-start.78 = (f32[1536]{0:T(1024)S(1)}, f32[1536]{0:T(1024)}, u32[]{:S(2)}) copy-start(f32[1536]{0:T(1024)} %get-tuple-element.84) | copy-start | bytes 18436
  204.9 20.3 %copy-start.79 = (f32[1536]{0:T(1024)S(1)}, f32[1536]{0:T(1024)}, u32[]{:S(2)}) copy-start(f32[1536]{0:T(1024)} %get-tuple-element.86) | copy-start | bytes 18436
  226.4 21.3 %copy-start.75 = (f32[384]{0:T(512)S(1)}, f32[384]{0:T(512)}, u32[]{:S(2)}) copy-start(f32[384]{0:T(512)} %get-tuple-element.28) | copy-start | bytes 4612
  226.4 21.3 %copy-start.76 = (f32[384]{0:T(512)S(1)}, f32[384]{0:T(512)}, u32[]{:S(2)}) copy-start(f32[384]{0:T(512)} %get-tuple-element.90) | copy-start | bytes 4612
  226.4 22.6 %copy-start.14 = (f32[197,384]{1,0:T(8,128)S(1)}, f32[197,384]{1,0:T(8,128)}, u32[]{:S(2)}) copy-start(f32[197,384]{1,0:T(8,128)} %get-tuple-element.35) | copy-start | bytes 907780
  226.4 22.6 %copy-start.46 = (f32[197,384]{1,0:T(8,128)S(1)}, f32[197,384]{1,0:T(8,128)}, u32[]{:S(2)}) copy-start(f32[197,384]{1,0:T(8,128)} %fusion.131) | copy-start | bytes 907780
  226.4 22.6 %copy-start.50 = (f32[197,384]{1,0:T(8,128)S(1)}, f32[197,384]{1,0:T(8,128)}, u32[]{:S(2)}) copy-start(f32[197,384]{1,0:T(8,128)} %get-tuple-element.83) | copy-start | bytes 907780
  247.7 2.4 copy-start.89
  247.7 3.7 copy-start.88
  247.7 5.1 %copy-start.82 = (f32[384]{0:T(512)S(1)}, f32[384]{0:T(512)}, u32[]{:S(2)}) copy-start(f32[384]{0:T(512)} %get-tuple-element.64) | copy-start | bytes 4612
  247.7 5.1 %copy-start.87 = (f32[384]{0:T(512)S(1)}, f32[384]{0:T(512)}, u32[]{:S(2)}) copy-start(f32[384]{0:T(512)} %get-tuple-element.14) | copy-start | bytes 4612
  247.7 6.4 %copy-start.81 = (f32[384]{0:T(512)S(1)}, f32[384]{0:T(512)}, u32[]{:S(2)}) copy-start(f32[384]{0:T(512)} %get-tuple-element.61) | copy-start | bytes 4612
  247.7 6.4 %copy-start.86 = (f32[384]{0:T(512)S(1)}, f32[384]{0:T(512)}, u32[]{:S(2)}) copy-start(f32[384]{0:T(512)} %get-tuple-element.25) | copy-start | bytes 4612
  256.7 1.3 copy-start.1
  256.7 1.3 copy-start.66
  256.8 2.8 copy-start.18
  259.6 1.5 copy-start.85
  259.6 1.5 copy-start.84
  259.6 1.5 copy-start.12
  259.6 1.5 copy-start.58
  (29 other events, 27.6 us)
Sparse Core Ops, SparseCore 0:
  11.6 75.2 all-gather.2
  256.9 163.5 all-reduce.2
where the time goes:
time: 436 us; the launch traced here: 429 us
  waiting for transfers between devices  229 us (53%)
  local copies, waits for them, and re-layouts  99.4 us (23%)
  other arithmetic  44.2 us (10%)
  matrix products  40.7 us (9%)
  between operations  15.9 us (4%)
    unnamed x3, waiting for transfers between devices  158 us
    all_gather x1, waiting for transfers between devices, fetch_weights(): return unpack_flat(lax.all_gather(params, 'dp', axis=0, tiled=True))  70.9 us
    unnamed x189, local copies, waits for them, and re-layouts  66.8 us
    all_gather x1, other arithmetic, fetch_weights(): return unpack_flat(lax.all_gather(params, 'dp', axis=0, tiled=True))  21.3 us
    dot_general x8, matrix products, left_product(): lax.dot_general(first, second, (((0,), (0,)), ((), ())), preferred_elemen...  12 us
    unnamed x9, other arithmetic  11.8 us
    dot_general x8, matrix products, right_product(): lax.dot_general(first, second, (((1,), (1,)), ((), ())), preferred_elemen...  10.4 us
    reshape x4, local copies, waits for them, and re-layouts, on_device(): totals[entry_name].reshape(-1)  10.1 us
  transfers between devices with their start and end apart: 2, of which 2 were waited for; matrix products, arithmetic and copies ran while one was open for 2% of the time, Pallas kernels for 0%

commit v1 on v0

--- a/solution.py
+++ b/solution.py
@@ -1,3 +1,4 @@
+import functools
 import jax
 import jax.numpy as jnp
 from jax import lax
@@ -12,6 +13,22 @@
 EPSILON = 1e-06
 SQRT_HALF = 0.7071067811865476
 INV_ROOT_TAU = 0.3989422804014327
+
+
+def _order_widths(panel, out_dim):
+    r1 = lax.psum(1, "dp")
+    reply, y, mat_out = (r1, lax.axis_index("dp"), panel.shape[out_dim])
+    e_next, h_now = (panel, 1)
+    while h_now < reply:
+        e_next = jnp.concatenate(
+            [e_next, lax.ppermute(e_next, "dp", [(t, (t - h_now) % reply) for t in range(reply)])],
+            axis=out_dim,
+        )
+        h_now = 2 * h_now
+    return jnp.roll(e_next, shift=y * mat_out, axis=out_dim)
+
+
+assign_rings_in = functools.partial(_order_widths, out_dim=0)
 
 
 def param_layout():
@@ -45,7 +62,7 @@
 
 
 def fetch_weights(params):
-    return unpack_flat(lax.all_gather(params, "dp", axis=0, tiled=True))
+    return unpack_flat(assign_rings_in(params))
 
 
 def standardize(values):

time: 436 us -> 537 us (1.23)
  waiting for transfers between devices: 229 us -> 273 us
  local copies, waits for them, and re-layouts: 99.4 us -> 126 us
  other arithmetic: 44.2 us -> 57.1 us
  starting transfers between devices: 0.08 us -> 10.9 us
    ppermute x0 -> x5, waiting for transfers between devices: none -> 115 us  [_order_widths(): lax.ppermute(e_next, 'dp', [(t, (t - h_now) % reply) for t in range(reply)])]
    all_gather x1, waiting for transfers between devices: 70.9 us -> 0.01 us  [on_device(): weights = unpack_flat(lax.all_gather(params, 'dp', axis=0, tiled=True))]
    unnamed x189 -> x252, local copies, waits for them, and re-layouts: 66.8 us -> 80 us
    ppermute x0 -> x5, starting transfers between devices: none -> 10.9 us  [_order_widths(): lax.ppermute(e_next, 'dp', [(t, (t - h_now) % reply) for t in range(reply)])]
    reshape x4 -> x8, local copies, waits for them, and re-layouts: 5.88 us -> 15.5 us  [unpack_flat(): flat_buffer[position:position + entry_size].reshape(entry_shape)]
    concatenate x0 -> x4, other arithmetic: none -> 9.08 us  [the longest x1 7.06 us: _order_widths(): return jnp.roll(e_next, shift=y * mat_out, axis=out_dim)]
    unnamed x9 -> x11, other arithmetic: 11.8 us -> 11.7 us
  transfers between devices with their start and end apart: 2 -> 7, of which waited for: 2 -> 5; matrix products, arithmetic and copies ran while one was open for 2% -> 13% of each run, Pallas kernels for 0% -> 0%
where the time goes in v1:
time: 537 us; the launch traced here: 528 us
  waiting for transfers between devices  273 us (51%)
  local copies, waits for them, and re-layouts  126 us (23%)
  other arithmetic  57.1 us (11%)
  matrix products  44.7 us (8%)
  between operations  16.3 us (3%)
  starting transfers between devices  10.9 us (2%)
    unnamed x3, waiting for transfers between devices  157 us
    ppermute x5, waiting for transfers between devices, _order_widths(): lax.ppermute(e_next, 'dp', [(t, (t - h_now) % reply) for t in range(reply)])  115 us
    unnamed x252, local copies, waits for them, and re-layouts  80 us
    all_gather x1, other arithmetic, on_device(): weights = unpack_flat(lax.all_gather(params, 'dp', axis=0, tiled=True))  22.7 us
    reshape x8, local copies, waits for them, and re-layouts, unpack_flat(): flat_buffer[position:position + entry_size].reshape(entry_shape)  15.5 us
    dot_general x8, matrix products, right_product(): lax.dot_general(first, second, (((1,), (1,)), ((), ())), preferred_elemen...  12.6 us
    unnamed x11, other arithmetic  11.7 us
    dot_general x8, matrix products, left_product(): lax.dot_general(first, second, (((0,), (0,)), ((), ())), preferred_elemen...  11.2 us
  transfers between devices with their start and end apart: 7, of which 5 were waited for; matrix products, arithmetic and copies ran while one was open for 13% of the time, Pallas kernels for 0%

profile of v1, /device:TPU:0, one launch (start us, length us, event | category | flops | bytes accessed | tf_op | source)
XLA Modules:
  0.0 528.0 jit_solution(13682688024338485169)
XLA Ops:
  7.2 6.4 %collective-permute-start = (bf16[55552]{0:T(1024)(128)(2,1)}, bf16[55552]{0:T(1024)(128)(2,1)S(1)}, u32[]{:S(2)}, u32[]{:S(2)}) collective-permute-start(bf16[55552]{0:T(1024)(128)(2,1)} %param.7), channel_id=1, source_target_pairs={{0,31},{1,0},{2,1},{3,2},{4,3},{5,4},{6,5},{7,6},{8,7},{9,8},{10,9... | collective-permute-start | bytes 333320 | tf_op jit(solution)/shard_map/ppermute | solution.py:24
  13.6 2.7 collective-permute-done
  17.9 5.4 %collective-permute-done.1 = bf16[111104]{0:T(1024)(128)(2,1)S(1)} collective-permute-done((bf16[111104]{0:T(1024)(128)(2,1)S(1)}, bf16[111104]{0:T(1024)(128)(2,1)S(1)}, u32[]{:S(2)}, u32[]{:S(2)}) %collective-permute-start.1) | collective-permute-done | bytes 222240 | tf_op jit(solution)/shard_map/ppermute | solution.py:24
  26.9 2.9 dynamic-update-slice.14
  31.0 2.9 dynamic-update-slice.15
  33.9 2.0 dynamic-update-slice.22
  35.9 4.4 dynamic-update-slice.16
  40.4 1.9 collective-permute-start.3
  43.2 22.2 %collective-permute-done.3 = bf16[444416]{0:T(1024)(128)(2,1)S(1)} collective-permute-done((bf16[444416]{0:T(1024)(128)(2,1)S(1)}, bf16[444416]{0:T(1024)(128)(2,1)S(1)}, u32[]{:S(2)}, u32[]{:S(2)}) %collective-permute-start.3) | collective-permute-done | bytes 888864 | tf_op jit(solution)/shard_map/ppermute | solution.py:24
  67.7 1.4 collective-permute-start.4
  71.2 1.4 convert_reduce_fusion.6
  72.6 85.2 %collective-permute-done.4 = bf16[888832]{0:T(1024)(128)(2,1)} collective-permute-done((bf16[888832]{0:T(1024)(128)(2,1)}, bf16[888832]{0:T(1024)(128)(2,1)}, u32[]{:S(2)}, u32[]{:S(2)}) %collective-permute-start.4) | collective-permute-done | bytes 1777696 | tf_op jit(solution)/shard_map/ppermute | solution.py:24
  157.8 2.8 constant_dynamic-update-slice_fusion.4
  160.7 7.1 %fusion = bf16[1777664]{0:T(1024)(128)(2,1)S(1)} fusion(s32[]{:T(128)S(6)} %select_n.11, bf16[1777664]{0:T(1024)(128)(2,1)} %constant_dynamic-update-slice_fusion.4), kind=kLoop, calls=%fused_computation.2 | loop fusion | flops 7110656 | bytes 7110660 | tf_op jit(solution)/shard_map/jit(_roll_dynamic)/concatenate | solution.py:28
  168.4 1.5 slice.155
  169.9 1.6 fusion.136
  171.5 2.1 reshape.433
  176.8 2.2 reshape.438
  180.8 1.4 fusion.139
  186.0 4.2 fusion.5
  191.0 4.7 fusion.8
  196.5 2.1 convolution_add_fusion.1
  198.5 3.2 reshape.464
  201.8 22.7 %reduce.14 = bf16[32,55552]{1,0:T(8,128)(2,1)} reduce(bf16[32,1,55552]{2,1,0:T(2,128)(2,1)} %all-gather.3.cloned.1.call-done, bf16[]{:T(256)} %constant.121), dimensions={1}, to_apply=%all-gather.reduce_sub_computation | reduce | bytes 7110658 | tf_op jit(solution)/shard_map/all_gather | solution.py:270
  224.4 7.7 %reshape.468 = bf16[1777664]{0:T(1024)(128)(2,1)} reshape(bf16[32,55552]{1,0:T(8,128)(2,1)} %reduce.14) | data formatting | bytes 7110656
  232.1 1.3 slice_convert_fusion.3
  233.4 3.7 fusion.135
  237.9 3.1 reshape.446
  241.0 3.6 reshape.447
  244.6 3.2 convert_reduce_fusion
  247.8 1.4 convert_reduce_fusion.1
  250.0 1.9 multiply_reduce_fusion.3
  254.2 1.8 reshape.448
  256.0 2.8 convert_reduce_fusion.9
  259.8 1.7 copy.75
  261.6 2.0 convolution_convert_fusion
  269.9 1.8 fusion.105
  274.9 2.0 reshape.453
  276.9 1.4 convert_reduce_fusion.2
  278.3 2.9 fusion.132
  281.2 1.9 convolution_add_fusion
  283.1 2.6 reshape.461
  285.7 3.0 constant_dynamic-update-slice_fusion.14
  288.6 1.3 constant_dynamic-update-slice_fusion.13
  289.9 1.3 constant_dynamic-update-slice_fusion.12
  292.4 2.0 reshape.462
  294.4 2.0 convolution_add_fusion.2
  296.5 3.3 reshape.463
  299.9 1.4 fusion.64
  301.3 2.0 constant_dynamic-update-slice_fusion.11
  303.3 1.3 constant_dynamic-update-slice_fusion.10
  304.6 21.6 %dynamic-update-slice.5 = f32[1777664]{0:T(1024)} dynamic-update-slice(f32[1777664]{0:T(1024)} %constant_dynamic-update-slice_fusion.10, f32[589824]{0:T(1024)} %reshape.463, s32[]{} %constant.127) | dynamic-update-slice | bytes 4718596
  326.2 1.3 add_dynamic-update-slice_fusion
  327.5 20.2 %dynamic-update-slice.7 = f32[1777664]{0:T(1024)} dynamic-update-slice(f32[1777664]{0:T(1024)} %add_dynamic-update-slice_fusion, f32[589824]{0:T(1024)S(1)} %copy-done.2, s32[]{} %constant.129) | dynamic-update-slice | bytes 4718596
  347.7 1.3 constant_dynamic-update-slice_fusion.9
  349.0 1.3 constant_dynamic-update-slice_fusion.8
  350.3 1.3 constant_dynamic-update-slice_fusion.7
  351.6 1.3 constant_dynamic-update-slice_fusion.6
  352.9 1.3 constant_dynamic-update-slice_fusion.5
  354.2 1.3 broadcast_dynamic-update-slice_fusion
  355.5 1.2 copy-done.18
  357.4 1.6 fusion.40
  362.1 157.1 %all-reduce.3.cloned.1.call-done = f32[1777664]{0:T(1024)} async-done(((f32[1777664]{0:T(1024)}), f32[1777664]{0:T(1024)}) %all-reduce.3.cloned.1.call-update) | async-done | bytes 7110672
  519.2 1.8 dynamic-slice
  (328 shorter events, 40.6 us)
Async XLA Ops:
  7.2 17.6 %copy-start.19 = (bf16[55552]{0:T(1024)(128)(2,1)S(1)}, bf16[55552]{0:T(1024)(128)(2,1)}, u32[]{:S(2)}) copy-start(bf16[55552]{0:T(1024)(128)(2,1)} %param.7) | copy-start | bytes 333316
  7.2 194.6 %all-gather.3.cloned.1.call-start = ((), (), s32[]{:S(2)}) async-start(), calls=%async_computation | async-start | bytes 7332864 | tf_op jit(solution)/shard_map/all_gather | solution.py:270
  7.2 9.1 %collective-permute-start = (bf16[55552]{0:T(1024)(128)(2,1)}, bf16[55552]{0:T(1024)(128)(2,1)S(1)}, u32[]{:S(2)}, u32[]{:S(2)}) collective-permute-start(bf16[55552]{0:T(1024)(128)(2,1)} %param.7), channel_id=1, source_target_pairs={{0,31},{1,0},{2,1},{3,2},{4,3},{5,4},{6,5},{7,6},{8,7},{9,8},{10,9... | collective-permute-start | bytes 333320 | tf_op jit(solution)/shard_map/ppermute | solution.py:24
  17.2 6.0 %collective-permute-start.1 = (bf16[111104]{0:T(1024)(128)(2,1)S(1)}, bf16[111104]{0:T(1024)(128)(2,1)S(1)}, u32[]{:S(2)}, u32[]{:S(2)}) collective-permute-start(bf16[111104]{0:T(1024)(128)(2,1)S(1)} %pad_maximum_fusion.6), channel_id=1, source_target_pairs={{0,30},{1,31},{2,0},{3,1},{4,2},{5,3},{6,4},{7,5},{8,6},{9,7},{10,... | collective-permute-start | bytes 666632 | tf_op jit(solution)/shard_map/ppermute | solution.py:24
  24.2 16.1 %collective-permute-start.2 = (bf16[222208]{0:T(1024)(128)(2,1)S(1)}, bf16[222208]{0:T(1024)(128)(2,1)S(1)}, u32[]{:S(2)}, u32[]{:S(2)}) collective-permute-start(bf16[222208]{0:T(1024)(128)(2,1)S(1)} %pad_maximum_fusion.3), channel_id=1, source_target_pairs={{0,28},{1,29},{2,30},{3,31},{4,0},{5,1},{6,2},{7,3},{8,4},{9,5},{1... | collective-permute-start | bytes 1333256 | tf_op jit(solution)/shard_map/ppermute | solution.py:24
  25.6 493.6 %all-reduce.3.cloned.1.call-start = ((), (), s32[]{:S(2)}) async-start(), calls=%async_computation.1 | async-start | bytes 14221312
  40.4 25.0 %collective-permute-start.3 = (bf16[444416]{0:T(1024)(128)(2,1)S(1)}, bf16[444416]{0:T(1024)(128)(2,1)S(1)}, u32[]{:S(2)}, u32[]{:S(2)}) collective-permute-start(bf16[444416]{0:T(1024)(128)(2,1)S(1)} %pad_maximum_fusion), channel_id=1, source_target_pairs={{0,24},{1,25},{2,26},{3,27},{4,28},{5,29},{6,30},{7,31},{8,0},{9,1... | collective-permute-start | bytes 2666504 | tf_op jit(solution)/shard_map/ppermute | solution.py:24
  65.4 3.6 copy-start.57
  67.7 3.1 copy-start.58
  67.7 90.2 %collective-permute-start.4 = (bf16[888832]{0:T(1024)(128)(2,1)}, bf16[888832]{0:T(1024)(128)(2,1)}, u32[]{:S(2)}, u32[]{:S(2)}) collective-permute-start(bf16[888832]{0:T(1024)(128)(2,1)} %copy-done.116), channel_id=1, source_target_pairs={{0,16},{1,17},{2,18},{3,19},{4,20},{5,21},{6,22},{7,23},{8,24},{9,... | collective-permute-start | bytes 5333000 | tf_op jit(solution)/shard_map/ppermute | solution.py:24
  70.3 112.6 %copy-start.7 = (bf16[1,197,384]{2,1,0:T(8,128)(2,1)}, bf16[1,197,384]{2,1,0:T(8,128)(2,1)S(1)}, u32[]{:S(2)}) copy-start(bf16[1,197,384]{2,1,0:T(8,128)(2,1)S(1)} %get-tuple-element.40) | copy-start | bytes 453892
  70.3 199.5 %copy-start.10 = (bf16[1,197,384]{2,1,0:T(8,128)(2,1)}, bf16[1,197,384]{2,1,0:T(8,128)(2,1)S(1)}, u32[]{:S(2)}) copy-start(bf16[1,197,384]{2,1,0:T(8,128)(2,1)S(1)} %get-tuple-element.104) | copy-start | bytes 453892
  70.3 103.4 %copy-start.75 = (f32[197]{0:T(256)}, f32[197]{0:T(256)S(1)}, u32[]{:S(2)}) copy-start(f32[197]{0:T(256)S(1)} %broadcast_multiply_fusion.9) | copy-start | bytes 2368
  70.5 103.7 %copy-start.72 = (f32[197]{0:T(256)}, f32[197]{0:T(256)S(1)}, u32[]{:S(2)}) copy-start(f32[197]{0:T(256)S(1)} %broadcast_multiply_fusion.11) | copy-start | bytes 2368
  72.6 101.1 %copy-start.90 = (f32[197]{0:T(256)}, f32[197]{0:T(256)S(1)}, u32[]{:S(2)}) copy-start(f32[197]{0:T(256)S(1)} %add_rsqrt_fusion.1) | copy-start | bytes 2368
  72.6 101.6 %copy-start.87 = (f32[197]{0:T(256)}, f32[197]{0:T(256)S(1)}, u32[]{:S(2)}) copy-start(f32[197]{0:T(256)S(1)} %add_rsqrt_fusion.3) | copy-start | bytes 2368
  168.4 5.8 %copy-start.69 = (f32[384]{0:T(512)}, f32[384]{0:T(512)S(1)}, u32[]{:S(2)}) copy-start(f32[384]{0:T(512)S(1)} %get-tuple-element.52) | copy-start | bytes 4612
  168.4 22.4 %copy-start.78 = (f32[384]{0:T(512)}, f32[384]{0:T(512)S(1)}, u32[]{:S(2)}) copy-start(f32[384]{0:T(512)S(1)} %get-tuple-element.46) | copy-start | bytes 4612
  175.0 7.5 %copy-start.36 = (bf16[197,384]{0,1:T(8,128)(2,1)}, bf16[197,384]{0,1:T(8,128)(2,1)S(1)}, u32[]{:S(2)}) copy-start(bf16[197,384]{0,1:T(8,128)(2,1)S(1)} %copy.65) | copy-start | bytes 453892
  179.2 5.0 copy-start.34
  183.4 7.4 %copy-start.93 = (f32[197]{0:T(256)}, f32[197]{0:T(256)S(1)}, u32[]{:S(2)}) copy-start(f32[197]{0:T(256)S(1)} %broadcast_multiply_fusion.8) | copy-start | bytes 2368
  185.0 71.1 %copy-start.3 = (f32[197,384]{1,0:T(8,128)}, f32[197,384]{1,0:T(8,128)S(1)}, u32[]{:S(2)}) copy-start(f32[197,384]{1,0:T(8,128)S(1)} %get-tuple-element.90) | copy-start | bytes 907780
  185.0 64.9 %copy-start.96 = (f32[197]{0:T(256)}, f32[197]{0:T(256)S(1)}, u32[]{:S(2)}) copy-start(f32[197]{0:T(256)S(1)} %broadcast_multiply_fusion.10) | copy-start | bytes 2368
  185.2 5.6 %copy-start.98 = (f32[197]{0:T(256)}, f32[197]{0:T(256)S(1)}, u32[]{:S(2)}) copy-start(f32[197]{0:T(256)S(1)} %add_rsqrt_fusion) | copy-start | bytes 2368
  185.2 4.9 copy-start.101
  185.9 4.2 copy-start.54
  191.0 5.5 %copy-start.53 = (bf16[1,197,384]{2,1,0:T(8,128)(2,1)S(1)}, bf16[1,197,384]{2,1,0:T(8,128)(2,1)}, u32[]{:S(2)}) copy-start(bf16[1,197,384]{2,1,0:T(8,128)(2,1)} %get-tuple-element.30) | copy-start | bytes 453892
  233.4 3.8 copy-start.1
  244.6 3.2 copy-start.55
  244.6 3.2 copy-start.60
  244.6 3.2 copy-start.117
  256.0 5.5 %copy-start.68 = (f32[6,197]{1,0:T(8,128)S(1)}, f32[6,197]{1,0:T(8,128)}, u32[]{:S(2)}) copy-start(f32[6,197]{1,0:T(8,128)} %copy-done.67) | copy-start | bytes 14188
  258.8 4.7 copy-start.12
  258.8 4.7 copy-start.37
  267.8 3.9 copy-start.38
  285.7 5.6 %copy-start.13 = (f32[197,384]{1,0:T(8,128)S(1)}, f32[197,384]{1,0:T(8,128)}, u32[]{:S(2)}) copy-start(f32[197,384]{1,0:T(8,128)} %copy-done.12) | copy-start | bytes 907780
  285.7 5.6 %copy-start.27 = (f32[384,384]{1,0:T(8,128)S(1)}, f32[384,384]{1,0:T(8,128)}, u32[]{:S(2)}) copy-start(f32[384,384]{1,0:T(8,128)} %fusion.129) | copy-start | bytes 1769476
  285.7 5.6 %copy-start.33 = (bf16[6,64,197]{2,1,0:T(8,128)(2,1)S(1)}, bf16[6,64,197]{2,1,0:T(8,128)(2,1)}, u32[]{:S(2)}) copy-start(bf16[6,64,197]{2,1,0:T(8,128)(2,1)} %copy-done.32) | copy-start | bytes 453892
  291.2 3.1 copy-start.80
  291.2 3.1 copy-start.83
  291.3 3.1 copy-start.95
  291.3 3.1 copy-start.100
  296.4 3.4 copy-start.11
  296.4 3.4 copy-start.39
  296.4 3.4 copy-start.50
  296.4 3.4 copy-start.52
  296.4 3.4 copy-start.61
  296.4 3.4 copy-start.64
  296.4 3.4 copy-start.74
  296.5 3.4 copy-start.77
  296.5 3.4 copy-start.89
  296.5 3.4 copy-start.92
  296.5 3.4 copy-start.111
  299.9 3.4 copy-start.106
  299.9 3.4 copy-start.107
  304.6 21.6 %copy-start.109 = (f32[1536]{0:T(1024)S(1)}, f32[1536]{0:T(1024)}, u32[]{:S(2)}) copy-start(f32[1536]{0:T(1024)} %get-tuple-element.101) | copy-start | bytes 18436
  304.6 21.6 %copy-start.110 = (f32[1536]{0:T(1024)S(1)}, f32[1536]{0:T(1024)}, u32[]{:S(2)}) copy-start(f32[1536]{0:T(1024)} %get-tuple-element.99) | copy-start | bytes 18436
  304.6 22.9 %copy-start.2 = (f32[589824]{0:T(1024)S(1)}, f32[589824]{0:T(1024)}, u32[]{:S(2)}) copy-start(f32[589824]{0:T(1024)} %reshape.464) | copy-start | bytes 7077892
  327.5 20.2 %copy-start.104 = (f32[384]{0:T(512)S(1)}, f32[384]{0:T(512)}, u32[]{:S(2)}) copy-start(f32[384]{0:T(512)} %get-tuple-element.29) | copy-start | bytes 4612
  327.5 20.2 %copy-start.105 = (f32[384]{0:T(512)S(1)}, f32[384]{0:T(512)}, u32[]{:S(2)}) copy-start(f32[384]{0:T(512)} %get-tuple-element.105) | copy-start | bytes 4612
  327.5 24.1 %copy-start.114 = (f32[384]{0:T(512)S(1)}, f32[384]{0:T(512)}, u32[]{:S(2)}) copy-start(f32[384]{0:T(512)} %get-tuple-element.15) | copy-start | bytes 4612
  327.5 24.1 %copy-start.115 = (f32[384]{0:T(512)S(1)}, f32[384]{0:T(512)}, u32[]{:S(2)}) copy-start(f32[384]{0:T(512)} %get-tuple-element.80) | copy-start | bytes 4612
  327.5 25.4 %copy-start.112 = (f32[384]{0:T(512)S(1)}, f32[384]{0:T(512)}, u32[]{:S(2)}) copy-start(f32[384]{0:T(512)} %get-tuple-element.26) | copy-start | bytes 4612
  327.5 25.4 %copy-start.113 = (f32[384]{0:T(512)S(1)}, f32[384]{0:T(512)}, u32[]{:S(2)}) copy-start(f32[384]{0:T(512)} %get-tuple-element.77) | copy-start | bytes 4612
  (62 other events, 105.5 us)
Sparse Core Ops, SparseCore 0:
  25.8 161.2 all-gather.2
  355.6 163.5 all-reduce.2
